TPU v7x, 32 devices: a whole 2x2x4 slice. The times are simulated.
32 devices in a mesh: dp: 4 (over y, x), vocab: 8 (over z, core).
Axes of the slice: x: 2, y: 2, z: 4, core: 2. Of those that a mesh axis runs over, the one named last changes fastest.
Arguments:
- hidden: bfloat16 [1024, 5120], P('dp')
- head_t: bfloat16 [5120, 19456], P('dp', 'vocab'), may hold values from -0.25 to 0.25
- targets: int32 [1024], P('dp'), may hold values from 0 to 19455
- token_ids: int32 [1024], P('dp'), may hold values from 0 to 19455, as said below
- embed_cot: bfloat16 [1024, 5120], P('dp'), may hold values from -6 to 6
Outputs:
- head_grad: bfloat16 [5120, 19456], P('dp', 'vocab')
- embed_grad: bfloat16 [5120, 19456], P('dp', 'vocab')
- hidden_grad: bfloat16 [1024, 5120], P('vocab', 'dp')
Inputs may be any that keep to these rules, and one draw needn't show every extreme that they name: `token_ids`: among the 256 input ids of one data group, at most 64 lie in any one block of 2432 vocabulary rows that starts at a multiple of 2432; in every group some block holds exactly 64.
All inputs are finite; a program needn't handle non-finite values.
Results may differ from a plain program's by a relative error of at most 0.0033.
Values may be sent and summed in bfloat16 or wider, within the bound.
A program may use at most 128 MiB of HBM per device.

v0:
```python
import jax
import jax.numpy as jnp
from jax import lax
from jax.sharding import PartitionSpec as P


def on_device(hidden, head_t, targets, token_ids, embed_cot):
    width_dev = head_t.shape[1]
    offset = lax.axis_index("vocab") * width_dev
    all_ids = lax.all_gather(token_ids, "dp", axis=0, tiled=True)
    columns = offset + jnp.arange(width_dev, dtype=jnp.int32)[None, :]
    local_hidden, local_cot = (
        lax.all_to_all(hidden, "dp", split_axis=1, concat_axis=0, tiled=True),
        lax.all_to_all(embed_cot, "dp", split_axis=1, concat_axis=0, tiled=True),
    )
    id_hot = (columns == all_ids[:, None]).astype(jnp.bfloat16)
    embed_grad = lax.dot_general(
        local_cot, id_hot, (((0,), (0,)), ((), ())), preferred_element_type=jnp.float32
    ).astype(jnp.bfloat16)
    logits = lax.psum_scatter(
        jnp.dot(local_hidden, head_t, preferred_element_type=jnp.float32),
        "dp",
        scatter_dimension=0,
        tiled=True,
    )
    row_max = lax.pmax(jnp.max(logits, axis=1, keepdims=True), "vocab")
    expo = jnp.exp(logits - row_max)
    row_sum = lax.psum(jnp.sum(expo, axis=1, keepdims=True), "vocab")
    target_hot = (columns == targets[:, None]).astype(jnp.float32)
    dlogits = (expo / row_sum - target_hot).astype(jnp.bfloat16)
    all_grads = lax.all_gather(dlogits, "dp", axis=0, tiled=True)
    head_grad = lax.dot_general(
        local_hidden, all_grads, (((0,), (0,)), ((), ())), preferred_element_type=jnp.float32
    ).astype(jnp.bfloat16)
    hidden_grad = lax.psum_scatter(
        lax.dot_general(
            all_grads, head_t, (((1,), (1,)), ((), ())), preferred_element_type=jnp.float32
        ),
        "vocab",
        scatter_dimension=0,
        tiled=True,
    ).astype(jnp.bfloat16)
    return (head_grad, embed_grad, hidden_grad)


def solution(mesh):
    placed = (P("dp", None), P("dp", "vocab"), P("dp"), P("dp"), P("dp", None))
    return jax.shard_map(
        on_device,
        mesh=mesh,
        in_specs=placed,
        out_specs=(P("dp", "vocab"), P("dp", "vocab"), P("vocab", "dp")),
        check_vma=False,
    )
```

profile of v0, /device:TPU:0, one launch (start us, length us, event | category | flops | bytes accessed | tf_op | source)
XLA Modules:
  0.0 358.3 jit_solution(14743323993973278830)
XLA Ops:
  7.2 4.4 %copy.18 = bf16[256,5120]{0,1:T(8,128)(2,1)} copy(bf16[256,5120]{1,0:T(8,128)(2,1)} %param.5) | data formatting | bytes 5242880 | tf_op args[0]
  11.6 36.2 %all_to_all.38 = bf16[256,4,1280]{0,2,1:T(8,128)(2,1)S(1)} all-to-all(bf16[256,4,1280]{0,2,1:T(8,128)(2,1)} %bitcast.22), channel_id=1, replica_groups=mesh['dp'=4,'vocab'=8] {'dp'}, dimensions={1} | all-to-all | bytes 5242880 | tf_op jit(solution)/shard_map/all_to_all | solution.py:13
  47.8 2.6 copy.19
  50.4 12.5 %fusion.8 = f32[1024,2432]{1,0:T(8,128)} fusion(bf16[1024,1280]{1,0:T(8,128)(2,1)} %bitcast.23, bf16[1280,2432]{1,0:T(8,128)(2,1)} %param.6), kind=kOutput, calls=%fused_computation.11 | convolution fusion | flops 6375342080 | bytes 18808832 | tf_op jit(solution)/shard_map/dot_general | solution.py:21
  62.9 0.0 all-gather.3.cloned.1.call-start
  63.0 99.1 %reduce-scatter.3.cloned.1.call-done = f32[256,2432]{1,0:T(8,128)} async-done(((f32[1024,2432]{1,0:T(8,128)}), f32[256,2432]{1,0:T(8,128)}) %reduce-scatter.3.cloned.1.call-update) | async-done | bytes 2490384 | tf_op jit(solution)/shard_map/reduce_scatter | solution.py:20
  162.1 2.1 reduce_max.9
  164.2 16.2 %pmax.7 = f32[256]{0:T(256)S(1)} all-reduce(f32[256]{0:T(256)S(1)} %reduce_max.9), channel_id=1, replica_groups=mesh['dp'=4,'vocab'=8] {'vocab'}, use_global_device_ids=true, to_apply=%region_2.0 | all-reduce | flops 256 | bytes 2048 | tf_op jit(solution)/shard_map/pmax | solution.py:26
  180.4 0.5 fusion.7
  180.9 13.6 %psum.7 = f32[256]{0:T(256)S(1)} all-reduce(f32[256]{0:T(256)S(1)} %fusion.7), channel_id=1, replica_groups=mesh['dp'=4,'vocab'=8] {'vocab'}, use_global_device_ids=true, to_apply=%region_4.0 | all-reduce | flops 256 | bytes 2048 | tf_op jit(solution)/shard_map/psum | solution.py:28
  194.5 1.8 subtract_convert_fusion
  196.3 0.0 reduce-scatter.5.cloned.1.call-start
  196.3 56.5 %all-gather.3.cloned.1.call-done = bf16[1024,2432]{1,0:T(8,128)(2,1)} async-done(((bf16[256,2432]{1,0:T(8,128)(2,1)}), bf16[1024,2432]{1,0:T(8,128)(2,1)}) %all-gather.3.cloned.1.call-update) | async-done | bytes 4980752 | tf_op jit(solution)/shard_map/all_gather | solution.py:31
  252.8 12.3 %fusion.9 = f32[1024,1280]{1,0:T(8,128)} fusion(bf16[1024,2432]{1,0:T(8,128)(2,1)} %all-gather.3.cloned.1.call-done, bf16[1280,2432]{1,0:T(8,128)(2,1)} %param.6), kind=kOutput, calls=%fused_computation.12 | convolution fusion | flops 6375342080 | bytes 16449536 | tf_op jit(solution)/shard_map/dot_general | solution.py:36
  265.0 1.7 copy-done.1
  266.8 2.5 copy.20
  269.3 3.8 %all-to-all-start.1 = ((bf16[256,4,1280]{0,2,1:T(8,128)(2,1)}), bf16[256,4,1280]{0,2,1:T(8,128)(2,1)S(1)}, u32[]{:S(2)}, u32[]{:S(2)}) async-start(bf16[256,4,1280]{0,2,1:T(8,128)(2,1)} %bitcast.20), calls=%async_computation.2 | async-start | bytes 5242880 | tf_op jit(solution)/shard_map/all_to_all | solution.py:14
  273.1 32.2 %all-gather = s32[4,1,256]{2,1,0:T(1,128)S(1)} all-gather(s32[1,1,256]{2,1,0:T(1,128)S(1)} %bitcast.27), channel_id=1, replica_groups=mesh['dp'=4,'vocab'=8] {'dp'}, dimensions={0}, use_global_device_ids=true | all-gather | bytes 5120 | tf_op jit(solution)/shard_map/all_gather | solution.py:10
  305.3 2.6 copy.21
  307.9 10.9 %fusion.2 = bf16[1280,2432]{0,1:T(8,128)(2,1)} fusion(bf16[1024,1280]{1,0:T(8,128)(2,1)} %bitcast.25, s32[2432]{0:T(1024)S(1)} %iota_add_fusion, s32[1024]{0:T(1024)S(1)} %bitcast.26), kind=kOutput, calls=%fused_computation.4 | convolution fusion | flops 6380945408 | bytes 8861184 | tf_op jit(solution)/shard_map/dot_general | solution.py:17
  318.7 9.5 %copy.23 = bf16[1280,2432]{1,0:T(8,128)(2,1)} copy(bf16[1280,2432]{0,1:T(8,128)(2,1)} %fusion.2) | data formatting | bytes 12451840
  328.2 12.3 %fusion.1 = bf16[1280,2432]{0,1:T(8,128)(2,1)} fusion(bf16[1024,2432]{1,0:T(8,128)(2,1)} %all-gather.3.cloned.1.call-done, bf16[1024,1280]{1,0:T(8,128)(2,1)S(1)} %bitcast.24), kind=kOutput, calls=%fused_computation.3 | convolution fusion | flops 6378455040 | bytes 13828096 | tf_op jit(solution)/shard_map/dot_general | solution.py:32
  340.6 9.3 %copy.22 = bf16[1280,2432]{1,0:T(8,128)(2,1)} copy(bf16[1280,2432]{0,1:T(8,128)(2,1)} %fusion.1) | data formatting | bytes 12451840
  349.9 1.8 convert_element_type.28
  (16 shorter events, 0.1 us)
Async XLA Ops:
  7.2 155.0 %reduce-scatter.3.cloned.1.call-start = ((), (), s32[]{:S(2)}) async-start(), calls=%async_computation.4 | async-start | bytes 12451840 | tf_op jit(solution)/shard_map/reduce_scatter | solution.py:20
  62.9 131.6 %copy-start.3 = (s32[256]{0:T(256)S(1)}, s32[256]{0:T(256)}, u32[]{:S(2)}) copy-start(s32[256]{0:T(256)} %param.7) | copy-start | bytes 3076
  62.9 189.8 %all-gather.3.cloned.1.call-start = ((), (), s32[]{:S(2)}) async-start(), calls=%async_computation.5 | async-start | bytes 6225920 | tf_op jit(solution)/shard_map/all_gather | solution.py:31
  162.1 18.3 %copy-start = (f32[256,2432]{1,0:T(8,128)S(1)}, f32[256,2432]{1,0:T(8,128)}, u32[]{:S(2)}) copy-start(f32[256,2432]{1,0:T(8,128)} %reduce-scatter.3.cloned.1.call-done) | copy-start | bytes 7471108
  196.3 153.6 %reduce-scatter.5.cloned.1.call-start = ((), (), s32[]{:S(2)}) async-start(), calls=%async_computation.6 | async-start | bytes 5898240 | tf_op jit(solution)/shard_map/reduce_scatter | solution.py:35
  265.0 1.7 copy-start.1
  269.3 3.8 %copy-start.4 = (s32[256]{0:T(256)S(1)}, s32[256]{0:T(256)}, u32[]{:S(2)}) copy-start(s32[256]{0:T(256)} %param.8) | copy-start | bytes 3076
  269.3 36.0 %all-to-all-start.1 = ((bf16[256,4,1280]{0,2,1:T(8,128)(2,1)}), bf16[256,4,1280]{0,2,1:T(8,128)(2,1)S(1)}, u32[]{:S(2)}, u32[]{:S(2)}) async-start(bf16[256,4,1280]{0,2,1:T(8,128)(2,1)} %bitcast.20), calls=%async_computation.2 | async-start | bytes 5242880 | tf_op jit(solution)/shard_map/all_to_all | solution.py:14
  318.7 9.5 %copy-start.2 = (bf16[4,256,1280]{2,1,0:T(8,128)(2,1)S(1)}, bf16[4,256,1280]{2,1,0:T(8,128)(2,1)}, u32[]{:S(2)}) copy-start(bf16[4,256,1280]{2,1,0:T(8,128)(2,1)} %copy.19) | copy-start | bytes 7864324
Sparse Core Ops, SparseCore 0:
  63.0 99.0 reduce-scatter.2
  196.4 56.3 all-gather.2
  265.2 59.8 reduce-scatter.4
where the time goes:
time: 359 us; the launch traced here: 358 us
  waiting for transfers between devices  156 us (43%)
  blocking collectives  98.2 us (27%)
  matrix products  48 us (13%)
  local copies, waits for them, and re-layouts  32.6 us (9%)
  between operations  13.8 us (4%)
  other arithmetic  6.14 us (2%)
  starting transfers between devices  3.93 us (1%)
    reduce_scatter x1, waiting for transfers between devices, on_device(): lax.psum_scatter(jnp.dot(local_hidden, head_t, preferred_element_type=jnp...  99.1 us
    all_gather x1, waiting for transfers between devices, on_device(): all_grads = lax.all_gather(dlogits, 'dp', axis=0, tiled=True)  56.5 us
    all_to_all x1, blocking collectives, on_device(): lax.all_to_all(hidden, 'dp', split_axis=1, concat_axis=0, tiled=True)  36.2 us
    all_gather x1, blocking collectives, on_device(): all_ids = lax.all_gather(token_ids, 'dp', axis=0, tiled=True)  32.2 us
    unnamed x14, local copies, waits for them, and re-layouts  27.5 us
    pmax x1, blocking collectives, on_device(): row_max = lax.pmax(jnp.max(logits, axis=1, keepdims=True), 'vocab')  16.2 us
    psum x1, blocking collectives, on_device(): row_sum = lax.psum(jnp.sum(expo, axis=1, keepdims=True), 'vocab')  13.6 us
    dot_general x1, matrix products, on_device(): jnp.dot(local_hidden, head_t, preferred_element_type=jnp.float32)  12.5 us
  transfers between devices with their start and end apart: 4, of which 2 were waited for; matrix products, arithmetic and copies ran while one was open for 13% of the time, Pallas kernels for 0%

commit v1 on v0

--- a/solution.py
+++ b/solution.py
@@ -10,7 +10,10 @@
     all_ids = lax.all_gather(token_ids, "dp", axis=0, tiled=True)
     columns = offset + jnp.arange(width_dev, dtype=jnp.int32)[None, :]
     local_hidden, local_cot = (
-        lax.all_to_all(hidden, "dp", split_axis=1, concat_axis=0, tiled=True),
+        jnp.concatenate(
+            lax.all_to_all(jnp.stack(jnp.split(hidden, lax.axis_size("dp"), axis=1)), "dp", 0, 0),
+            axis=0,
+        ),
         lax.all_to_all(embed_cot, "dp", split_axis=1, concat_axis=0, tiled=True),
     )
     id_hot = (columns == all_ids[:, None]).astype(jnp.bfloat16)

time: 359 us -> 342 us (0.953)
  local copies, waits for them, and re-layouts: 32.6 us -> 19.9 us
  matrix products: 48 us -> 43.6 us
    unnamed x14 -> x18, local copies, waits for them, and re-layouts: 27.5 us -> 15.3 us
  transfers between devices with their start and end apart: 4 -> 4, of which waited for: 2 -> 2; matrix products, arithmetic and copies ran while one was open for 13% -> 11% of each run, Pallas kernels for 0% -> 0%
where the time goes in v1:
time: 342 us; the launch traced here: 341 us
  waiting for transfers between devices  155 us (45%)
  blocking collectives  98.1 us (29%)
  matrix products  43.6 us (13%)
  local copies, waits for them, and re-layouts  19.9 us (6%)
  between operations  13.8 us (4%)
  other arithmetic  6.47 us (2%)
  starting transfers between devices  3.93 us (1%)
    reduce_scatter x1, waiting for transfers between devices, on_device(): lax.psum_scatter(jnp.dot(local_hidden, head_t, preferred_element_type=jnp...  99 us
    all_gather x1, waiting for transfers between devices, on_device(): all_grads = lax.all_gather(dlogits, 'dp', axis=0, tiled=True)  56.5 us
    all_to_all x1, blocking collectives, on_device(): lax.all_to_all(jnp.stack(jnp.split(hidden, lax.axis_size('dp'), axis=1)),...  36.1 us
    all_gather x1, blocking collectives, on_device(): all_ids = lax.all_gather(token_ids, 'dp', axis=0, tiled=True)  32.2 us
    pmax x1, blocking collectives, on_device(): row_max = lax.pmax(jnp.max(logits, axis=1, keepdims=True), 'vocab')  16.2 us
    unnamed x18, local copies, waits for them, and re-layouts  15.3 us
    psum x1, blocking collectives, on_device(): row_sum = lax.psum(jnp.sum(expo, axis=1, keepdims=True), 'vocab')  13.6 us
    dot_general x1, matrix products, on_device(): lax.dot_general(all_grads, head_t, (((1,), (1,)), ((), ())), preferred_el...  12.2 us
  transfers between devices with their start and end apart: 4, of which 2 were waited for; matrix products, arithmetic and copies ran while one was open for 11% of the time, Pallas kernels for 0%

profile of v1, /device:TPU:0, one launch (start us, length us, event | category | flops | bytes accessed | tf_op | source)
XLA Modules:
  0.0 341.3 jit_solution(13375268797704114774)
XLA Ops:
  7.2 2.0 slice_bitcast_fusion.3
  9.2 0.3 pad_maximum_fusion
  9.6 36.1 %all_to_all.24 = bf16[4,256,1280]{2,1,0:T(8,128)(2,1)S(1)} all-to-all(bf16[4,256,1280]{2,1,0:T(8,128)(2,1)S(1)} %pad_maximum_fusion), channel_id=1, replica_groups=mesh['dp'=4,'vocab'=8] {'dp'}, dimensions={0} | all-to-all | bytes 5242880 | tf_op jit(solution)/shard_map/all_to_all | solution.py:14
  45.7 1.5 copy-done.2
  47.2 9.3 %fusion.7 = f32[1024,2432]{1,0:T(8,128)} fusion(bf16[1024,1280]{1,0:T(8,128)(2,1)S(1)} %bitcast.25, bf16[1280,2432]{1,0:T(8,128)(2,1)S(1)} %bitcast.31), kind=kOutput, calls=%fused_computation.15 | convolution fusion | flops 6375342080 | bytes 18808832 | tf_op jit(solution)/shard_map/dot_general | solution.py:24
  56.5 0.0 all-gather.3.cloned.1.call-start
  56.6 99.0 %reduce-scatter.3.cloned.1.call-done = f32[256,2432]{1,0:T(8,128)} async-done(((f32[1024,2432]{1,0:T(8,128)}), f32[256,2432]{1,0:T(8,128)}) %reduce-scatter.3.cloned.1.call-update) | async-done | bytes 2490384 | tf_op jit(solution)/shard_map/reduce_scatter | solution.py:23
  155.6 2.1 reduce_max.9
  157.6 16.2 %pmax.7 = f32[256]{0:T(256)S(1)} all-reduce(f32[256]{0:T(256)S(1)} %reduce_max.9), channel_id=1, replica_groups=mesh['dp'=4,'vocab'=8] {'vocab'}, use_global_device_ids=true, to_apply=%region_2.0 | all-reduce | flops 256 | bytes 2048 | tf_op jit(solution)/shard_map/pmax | solution.py:29
  173.8 0.5 fusion.6
  174.3 13.6 %psum.7 = f32[256]{0:T(256)S(1)} all-reduce(f32[256]{0:T(256)S(1)} %fusion.6), channel_id=1, replica_groups=mesh['dp'=4,'vocab'=8] {'vocab'}, use_global_device_ids=true, to_apply=%region_4.0 | all-reduce | flops 256 | bytes 2048 | tf_op jit(solution)/shard_map/psum | solution.py:31
  187.9 1.8 subtract_convert_fusion
  189.7 0.0 reduce-scatter.5.cloned.1.call-start
  189.7 56.5 %all-gather.3.cloned.1.call-done = bf16[1024,2432]{1,0:T(8,128)(2,1)} async-done(((bf16[256,2432]{1,0:T(8,128)(2,1)}), bf16[1024,2432]{1,0:T(8,128)(2,1)}) %all-gather.3.cloned.1.call-update) | async-done | bytes 4980752 | tf_op jit(solution)/shard_map/all_gather | solution.py:34
  246.2 12.2 %fusion.8 = f32[1024,1280]{1,0:T(8,128)} fusion(bf16[1024,2432]{1,0:T(8,128)(2,1)} %all-gather.3.cloned.1.call-done, bf16[1280,2432]{1,0:T(8,128)(2,1)} %param.6), kind=kOutput, calls=%fused_computation.16 | convolution fusion | flops 6375342080 | bytes 16449536 | tf_op jit(solution)/shard_map/dot_general | solution.py:39
  258.4 1.7 copy-done.1
  260.1 2.5 copy.13
  262.7 3.8 %all-to-all-start.1 = ((bf16[256,4,1280]{0,2,1:T(8,128)(2,1)}), bf16[256,4,1280]{0,2,1:T(8,128)(2,1)S(1)}, u32[]{:S(2)}, u32[]{:S(2)}) async-start(bf16[256,4,1280]{0,2,1:T(8,128)(2,1)} %bitcast.24), calls=%async_computation.2 | async-start | bytes 5242880 | tf_op jit(solution)/shard_map/all_to_all | solution.py:17
  266.5 32.2 %all-gather = s32[4,1,256]{2,1,0:T(1,128)S(1)} all-gather(s32[1,1,256]{2,1,0:T(1,128)S(1)} %bitcast.29), channel_id=1, replica_groups=mesh['dp'=4,'vocab'=8] {'dp'}, dimensions={0}, use_global_device_ids=true | all-gather | bytes 5120 | tf_op jit(solution)/shard_map/all_gather | solution.py:10
  298.7 2.6 copy.14
  301.2 10.9 %fusion.1 = bf16[1280,2432]{0,1:T(8,128)(2,1)} fusion(bf16[1024,1280]{1,0:T(8,128)(2,1)} %bitcast.27, s32[2432]{0:T(1024)S(1)} %iota_add_fusion, s32[1024]{0:T(1024)S(1)} %bitcast.28), kind=kOutput, calls=%fused_computation.3 | convolution fusion | flops 6380945408 | bytes 8861184 | tf_op jit(solution)/shard_map/dot_general | solution.py:20
  312.1 9.5 %copy.15 = bf16[1280,2432]{1,0:T(8,128)(2,1)} copy(bf16[1280,2432]{0,1:T(8,128)(2,1)} %fusion.1) | data formatting | bytes 12451840
  321.6 11.3 %convolution_convert_fusion.1 = bf16[1280,2432]{1,0:T(8,128)(2,1)} fusion(bf16[1024,1280]{1,0:T(8,128)(2,1)S(1)} %bitcast.26, bf16[1024,2432]{1,0:T(8,128)(2,1)} %all-gather.3.cloned.1.call-done), kind=kOutput, calls=%fused_computation.1 | convolution fusion | flops 6378455040 | bytes 13828096 | tf_op jit(solution)/shard_map/dot_general | solution.py:35
  332.9 1.8 convert_element_type.24
  (22 shorter events, 0.1 us)
Async XLA Ops:
  7.2 148.4 %reduce-scatter.3.cloned.1.call-start = ((), (), s32[]{:S(2)}) async-start(), calls=%async_computation.4 | async-start | bytes 12451840 | tf_op jit(solution)/shard_map/reduce_scatter | solution.py:23
  7.2 40.0 %slice-start = ((s8[6225920]{0:T(1024)(128)(4,1)}), s8[4194304]{0:T(1024)(128)(4,1)S(1)}, s32[]{:S(2)}) async-start(s8[6225920]{0:T(1024)(128)(4,1)} %bitcast.30), calls=%async_computation.7 | async-start | bytes 8388608
  9.2 38.0 %slice-start.1 = ((s8[6225920]{0:T(1024)(128)(4,1)}), s8[2031616]{0:T(1024)(128)(4,1)S(1)}, s32[]{:S(2)}) async-start(s8[6225920]{0:T(1024)(128)(4,1)} %bitcast.30), calls=%async_computation.8 | async-start | bytes 4063232
  45.7 1.5 copy-start.2
  56.5 131.4 %copy-start.4 = (s32[256]{0:T(256)S(1)}, s32[256]{0:T(256)}, u32[]{:S(2)}) copy-start(s32[256]{0:T(256)} %param.7) | copy-start | bytes 3076
  56.5 189.6 %all-gather.3.cloned.1.call-start = ((), (), s32[]{:S(2)}) async-start(), calls=%async_computation.5 | async-start | bytes 6225920 | tf_op jit(solution)/shard_map/all_gather | solution.py:34
  155.6 18.3 %copy-start = (f32[256,2432]{1,0:T(8,128)S(1)}, f32[256,2432]{1,0:T(8,128)}, u32[]{:S(2)}) copy-start(f32[256,2432]{1,0:T(8,128)} %reduce-scatter.3.cloned.1.call-done) | copy-start | bytes 7471108
  189.7 143.2 %reduce-scatter.5.cloned.1.call-start = ((), (), s32[]{:S(2)}) async-start(), calls=%async_computation.6 | async-start | bytes 5898240 | tf_op jit(solution)/shard_map/reduce_scatter | solution.py:38
  258.4 1.7 copy-start.1
  262.7 3.8 %copy-start.5 = (s32[256]{0:T(256)S(1)}, s32[256]{0:T(256)}, u32[]{:S(2)}) copy-start(s32[256]{0:T(256)} %param.8) | copy-start | bytes 3076
  262.7 36.0 %all-to-all-start.1 = ((bf16[256,4,1280]{0,2,1:T(8,128)(2,1)}), bf16[256,4,1280]{0,2,1:T(8,128)(2,1)S(1)}, u32[]{:S(2)}, u32[]{:S(2)}) async-start(bf16[256,4,1280]{0,2,1:T(8,128)(2,1)} %bitcast.24), calls=%async_computation.2 | async-start | bytes 5242880 | tf_op jit(solution)/shard_map/all_to_all | solution.py:17
  312.1 9.5 %copy-start.3 = (bf16[4,256,1280]{2,1,0:T(8,128)(2,1)S(1)}, bf16[4,256,1280]{2,1,0:T(8,128)(2,1)}, u32[]{:S(2)}) copy-start(bf16[4,256,1280]{2,1,0:T(8,128)(2,1)} %copy-done.2) | copy-start | bytes 7864324
Sparse Core Ops, SparseCore 0:
  56.7 98.8 reduce-scatter.2
  189.8 56.3 all-gather.2
  258.5 59.8 reduce-scatter.4
